TPU v7x, 32 devices: a whole 2x2x4 slice. The times are simulated.
32 devices in a mesh: dp: 4 (over z), mp: 8 (over y, x, core).
Axes of the slice: x: 2, y: 2, z: 4, core: 2. Of those that a mesh axis runs over, the one named last changes fastest.
Arguments:
- hidden_in: bfloat16 [64, 8192], P(None, 'dp'), may hold values from -25 to 25
- norm_gain: bfloat16 [8192], P('dp'), may hold values from 0.099609375 to 1.8984375
- w_query: bfloat16 [8192, 8192], P('dp', 'mp'), may hold values from -0.0625 to 0.0625
- w_keyval: bfloat16 [8192, 2048], P('dp', 'mp'), may hold values from -0.25 to 0.25
- w_out: bfloat16 [8192, 8192], P('mp', 'dp'), may hold values from -0.5 to 0.5
- cache_slots: bfloat16 [2, 64, 2, 8, 512, 128], P(None, ('dp', 'mp')), may hold values from -140 to 140
- lengths: int32 [64], replicated, may hold values from 1 to 512, 16384 in all
- positions: int32 [64], replicated, may hold values from 0 to 8191
- slot_order: int32 [64], replicated, may hold values from 0 to 63, each once
Outputs:
- result: bfloat16 [64, 8192], P(None, 'dp')
Inputs may be any that keep to these rules, and one draw needn't show every extreme that they name: `lengths`: every request has at least one valid cache position; the longest has 512. `slot_order`: each request's cache sits in exactly one slot.
All inputs are finite; a program needn't handle non-finite values.
Results may differ from a plain program's by a relative error of at most 0.035.
Values may be sent and summed in bfloat16 or wider, within the bound.
A program may use at most 128 MiB of HBM per device.

v0:
```python
import math
import jax
import jax.numpy as jnp
from jax import lax
from jax.sharding import PartitionSpec as P

LAYERS = 2
norm_eps = 1e-05
rope_base = 500000.0


def rotate(values, at_positions):
    half_dim = values.shape[-1] // 2
    index_row = jnp.arange(half_dim, dtype=jnp.float32)
    frequency = jnp.exp(index_row * (-2.0 * math.log(rope_base) / values.shape[-1]))
    angles = at_positions.astype(jnp.float32)[:, None, None] * frequency
    cosines = jnp.cos(angles)
    sine_rows = jnp.sin(angles)
    first_half = values[..., :half_dim]
    second_half = values[..., half_dim:]
    return jnp.concatenate(
        [
            first_half * cosines - second_half * sine_rows,
            second_half * cosines + first_half * sine_rows,
        ],
        axis=-1,
    )


def attend(queries, fresh_keys, fresh_values, key_rows, values, slot_lengths):
    score_scale = 1.0 / math.sqrt(queries.shape[-1])
    scores = (
        jnp.einsum("rkgd,rktd->rkgt", queries, key_rows, preferred_element_type=jnp.float32)
        * score_scale
    )
    own_score = (
        jnp.einsum("rkgd,rkd->rkg", queries, fresh_keys, preferred_element_type=jnp.float32)
        * score_scale
    )
    positions_row = lax.broadcasted_iota(jnp.int32, (1, 1, 1, key_rows.shape[2]), 3)
    valid_keys = positions_row < slot_lengths[:, None, None, None]
    scores = jnp.where(valid_keys, scores, -jnp.inf)
    highest = jnp.maximum(jnp.max(scores, axis=-1), own_score)
    weights = jnp.exp(scores - highest[..., None])
    own_weight = jnp.exp(own_score - highest)
    denominator = jnp.sum(weights, axis=-1) + own_weight
    rounded = weights.astype(jnp.bfloat16)
    own_rounded = lax.optimization_barrier(own_weight.astype(jnp.bfloat16)).astype(jnp.float32)
    summed = jnp.einsum("rkgt,rktd->rkgd", rounded, values, preferred_element_type=jnp.float32)
    summed = summed + own_rounded[..., None] * fresh_values.astype(jnp.float32)[:, :, None, :]
    return (summed / denominator[..., None]).astype(jnp.bfloat16)


def shards(
    hidden_in, norm_gain, w_query, w_keyval, w_out, cache_slots, lengths, positions, slot_order
):
    total_rows = hidden_in.shape[0]
    data_count = lax.axis_size("dp")
    model_count = lax.axis_size("mp")
    owned_rows = cache_slots.shape[1]
    key_heads = cache_slots.shape[3]
    head_dim = cache_slots.shape[5]
    query_cols = w_query.shape[1]
    head_count = query_cols * model_count // head_dim
    group_size = head_count // key_heads
    model_width = hidden_in.shape[1] * data_count
    half_width = key_heads * head_dim
    inverse = (
        jnp.zeros((total_rows,), jnp.int32)
        .at[slot_order]
        .set(jnp.arange(total_rows, dtype=jnp.int32))
    )
    device_index = lax.axis_index("dp") * model_count + lax.axis_index("mp")
    slot_lengths = lax.dynamic_slice_in_dim(
        jnp.take(lengths, slot_order), device_index * owned_rows, owned_rows
    )
    slot_positions = lax.dynamic_slice_in_dim(
        jnp.take(positions, slot_order), device_index * owned_rows, owned_rows
    )
    gain_float = norm_gain.astype(jnp.float32)
    current = jnp.take(hidden_in, slot_order, axis=0)
    for layer_index in range(LAYERS):
        floats = current.astype(jnp.float32)
        squares = jnp.sum(floats * floats, axis=1)
        scaled = (floats * gain_float).astype(jnp.bfloat16)
        partial_value = jnp.concatenate(
            [
                jnp.dot(scaled, w_query, preferred_element_type=jnp.float32),
                jnp.dot(scaled, w_keyval, preferred_element_type=jnp.float32),
            ],
            axis=1,
        )
        summed = lax.psum_scatter(partial_value, "dp", scatter_dimension=0, tiled=True)
        square_sum = lax.psum_scatter(squares, "dp", scatter_dimension=0, tiled=True)
        inverse_rms = lax.rsqrt(square_sum / model_width + norm_eps)
        projected = summed * inverse_rms[:, None]
        arrived = lax.all_to_all(projected, "mp", split_axis=0, concat_axis=1, tiled=True)
        arrived = arrived.reshape(owned_rows, model_count, projected.shape[1])
        query_part = arrived[:, :, :query_cols].reshape(owned_rows, head_count, head_dim)
        keyval_part = arrived[:, :, query_cols:].reshape(owned_rows, 2 * half_width)
        queries = (
            rotate(query_part, slot_positions)
            .astype(jnp.bfloat16)
            .reshape(owned_rows, key_heads, group_size, head_dim)
        )
        fresh_keys = rotate(
            keyval_part[:, :half_width].reshape(owned_rows, key_heads, head_dim), slot_positions
        ).astype(jnp.bfloat16)
        fresh_values = (
            keyval_part[:, half_width:]
            .reshape(owned_rows, key_heads, head_dim)
            .astype(jnp.bfloat16)
        )
        layer_cache = cache_slots[layer_index]
        attended = attend(
            queries, fresh_keys, fresh_values, layer_cache[:, 0], layer_cache[:, 1], slot_lengths
        )
        attended = attended.reshape(owned_rows, head_count * head_dim)
        returned = lax.all_to_all(attended, "mp", split_axis=1, concat_axis=0, tiled=True)
        partial_out = jnp.dot(
            lax.all_gather(returned, "dp", axis=0, tiled=True),
            w_out,
            preferred_element_type=jnp.float32,
        )
        totals = lax.psum(partial_out, "mp")
        current = (floats + totals).astype(jnp.bfloat16)
    return jnp.take(current, inverse, axis=0)


def solution(mesh):
    placed = (
        P(None, "dp"),
        P("dp"),
        P("dp", "mp"),
        P("dp", "mp"),
        P("mp", "dp"),
        P(None, ("dp", "mp"), None, None, None, None),
        P(),
        P(),
        P(),
    )
    return jax.shard_map(
        shards, mesh=mesh, in_specs=placed, out_specs=P(None, "dp"), check_vma=False
    )
```

profile of v0, /device:TPU:0, one launch (start us, length us, event | category | flops | bytes accessed | tf_op | source)
XLA Modules:
  0.0 262.7 jit_solution(91832775183974861)
XLA Ops:
  12.4 3.1 %fusion.30 = f32[64,1024]{1,0:T(8,128)S(1)} fusion(bf16[2048,1024]{1,0:T(8,128)(2,1)} %param.15, f32[2048]{0:T(1024)S(1)} %convert_element_type.90, bf16[64,2048]{1,0:T(8,128)(2,1)S(1)} %gather_fusion, pred[64]{0:T(512)(128)(4,1)S(1)} %get-tuple-element.10), kind=kOutput, calls=%fused_computation.50 | convolution fusion | flops 268959744 | bytes 4726848 | tf_op jit(solution)/shard_map/dot_general | solution.py:88
  16.5 5.9 %fusion.59 = (bf16[1,2,2,8,512,128]{5,4,3,2,1,0:T(8,128)(2,1)}, bf16[1,2,2,8,512,128]{5,4,3,2,1,0:T(8,128)(2,1)}) fusion(bf16[2,2,2,8,512,128]{5,4,3,2,1,0:T(8,128)(2,1)} %param.18), kind=kLoop, calls=%fused_computation.118 | loop fusion | bytes 16777216 | tf_op jit(solution)/shard_map/slice | solution.py:114
  22.4 13.4 %all-reduce = f32[64]{0:T(128)S(1)} all-reduce(f32[64]{0:T(128)S(1)} %fusion.15), channel_id=3, replica_groups=mesh['dp'=4,'mp'=8] {'dp'}, use_global_device_ids=true, to_apply=%region_2.0.clone | all-reduce | flops 64 | bytes 512
  38.2 5.9 %copy_bitcast_fusion = (bf16[2,2,8,512,128]{4,3,2,0,1:T(8,128)(2,1)}, bf16[2,2,8,512,128]{4,3,2,0,1:T(8,128)(2,1)}) fusion(bf16[1,2,2,8,512,128]{5,4,3,2,1,0:T(8,128)(2,1)} %get-tuple-element.12, bf16[1,2,2,8,512,128]{5,4,3,2,1,0:T(8,128)(2,1)} %get-tuple-element.11), kind=kLoop, calls=%fused_computation.5 | loop fusion | bytes 16777216 | tf_op jit(solution)/shard_map/squeeze | solution.py:114
  45.8 3.7 %all-to-all-start = ((f32[8,2,1280]{2,1,0:T(2,128)}), f32[8,2,1280]{2,1,0:T(2,128)S(1)}, u32[]{:S(2)}, u32[]{:S(2)}) async-start(f32[8,2,1280]{2,1,0:T(2,128)} %all_to_all.52), calls=%async_computation.1 | async-start | bytes 163840 | tf_op jit(solution)/shard_map/all_to_all | solution.py:97
  49.6 5.0 %all-to-all-done = f32[8,2,1280]{2,1,0:T(2,128)S(1)} async-done(((f32[8,2,1280]{2,1,0:T(2,128)}), f32[8,2,1280]{2,1,0:T(2,128)S(1)}, u32[]{:S(2)}, u32[]{:S(2)}) %all-to-all-start) | async-done | bytes 81952 | tf_op jit(solution)/shard_map/all_to_all | solution.py:97
  55.2 2.4 fusion.60
  57.8 2.0 fusion.13
  59.9 7.2 %all_to_all.70 = bf16[2,8,1024]{2,0,1:T(2,128)(2,1)S(1)} all-to-all(bf16[2,8,1024]{2,0,1:T(2,128)(2,1)S(1)} %copy.21), channel_id=1, replica_groups=mesh['dp'=4,'mp'=8] {'mp'}, dimensions={1} | all-to-all | bytes 65536 | tf_op jit(solution)/shard_map/all_to_all | solution.py:119
  67.2 13.5 %all_gather.6 = bf16[64,1024]{1,0:T(8,128)(2,1)S(1)} all-gather(bf16[16,1024]{1,0:T(8,128)(2,1)S(1)} %all_to_all.58), channel_id=1, replica_groups=mesh['dp'=4,'mp'=8] {'dp'}, dimensions={0}, use_global_device_ids=true | all-gather | bytes 163840 | tf_op jit(solution)/shard_map/all_gather | solution.py:121
  80.7 3.9 %fusion.62 = f32[64,2048]{1,0:T(8,128)} fusion(bf16[64,1024]{1,0:T(8,128)(2,1)S(1)} %all_gather.6, bf16[1024,2048]{1,0:T(8,128)(2,1)} %param.17), kind=kOutput, calls=%fused_computation.121 | convolution fusion | flops 268435456 | bytes 4849664 | tf_op jit(solution)/shard_map/dot_general | solution.py:120
  84.6 51.1 %all-reduce.5.cloned.1.call-done = f32[64,2048]{1,0:T(8,128)} async-done(((f32[64,2048]{1,0:T(8,128)}), f32[64,2048]{1,0:T(8,128)}) %all-reduce.5.cloned.1.call-update) | async-done | bytes 524304 | tf_op jit(solution)/shard_map/psum | solution.py:125
  137.3 3.0 %fusion.26 = f32[64,1024]{1,0:T(8,128)S(1)} fusion(bf16[2048,1024]{1,0:T(8,128)(2,1)} %param.15, bf16[64,2048]{1,0:T(8,128)(2,1)S(1)} %get-tuple-element.8, f32[2048]{0:T(1024)S(1)} %convert_element_type.90), kind=kOutput, calls=%fused_computation.48 | convolution fusion | flops 268828672 | bytes 4726784 | tf_op jit(solution)/shard_map/dot_general | solution.py:88
  141.1 11.7 %all-reduce.1 = f32[64]{0:T(128)S(1)} all-reduce(f32[64]{0:T(128)S(1)} %get-tuple-element.6), channel_id=5, replica_groups=mesh['dp'=4,'mp'=8] {'dp'}, use_global_device_ids=true, to_apply=%region_8.11.clone | all-reduce | flops 64 | bytes 512
  152.9 7.7 %reduce-scatter.5.cloned.1.call-done = f32[16,1280]{1,0:T(8,128)} async-done(((f32[64,1280]{1,0:T(8,128)}), f32[16,1280]{1,0:T(8,128)}) %reduce-scatter.5.cloned.1.call-update) | async-done | bytes 81936 | tf_op jit(solution)/shard_map/reduce_scatter | solution.py:93
  162.3 3.7 %all-to-all-start.2 = ((f32[8,2,1280]{2,1,0:T(2,128)}), f32[8,2,1280]{2,1,0:T(2,128)S(1)}, u32[]{:S(2)}, u32[]{:S(2)}) async-start(f32[8,2,1280]{2,1,0:T(2,128)} %all_to_all.59), calls=%async_computation.4 | async-start | bytes 163840 | tf_op jit(solution)/shard_map/all_to_all | solution.py:97
  166.7 4.3 %all-to-all-done.2 = f32[8,2,1280]{2,1,0:T(2,128)S(1)} async-done(((f32[8,2,1280]{2,1,0:T(2,128)}), f32[8,2,1280]{2,1,0:T(2,128)S(1)}, u32[]{:S(2)}, u32[]{:S(2)}) %all-to-all-start.2) | async-done | bytes 81952 | tf_op jit(solution)/shard_map/all_to_all | solution.py:97
  171.4 2.4 fusion.61
  174.2 2.0 fusion.12
  176.9 3.3 %all-to-all-start.3 = ((bf16[2,8,1024]{2,0,1:T(2,128)(2,1)}), bf16[2,8,1024]{2,0,1:T(2,128)(2,1)S(1)}, u32[]{:S(2)}, u32[]{:S(2)}) async-start(bf16[2,8,1024]{2,0,1:T(2,128)(2,1)} %copy.24), calls=%async_computation.5 | async-start | bytes 65536 | tf_op jit(solution)/shard_map/all_to_all | solution.py:119
  180.3 4.7 %all-to-all-done.3 = bf16[2,8,1024]{2,0,1:T(2,128)(2,1)S(1)} async-done(((bf16[2,8,1024]{2,0,1:T(2,128)(2,1)}), bf16[2,8,1024]{2,0,1:T(2,128)(2,1)S(1)}, u32[]{:S(2)}, u32[]{:S(2)}) %all-to-all-start.3) | async-done | bytes 32800 | tf_op jit(solution)/shard_map/all_to_all | solution.py:119
  185.1 13.5 %all_gather.7 = bf16[64,1024]{1,0:T(8,128)(2,1)S(1)} all-gather(bf16[16,1024]{1,0:T(8,128)(2,1)S(1)} %all_to_all.65), channel_id=1, replica_groups=mesh['dp'=4,'mp'=8] {'dp'}, dimensions={0}, use_global_device_ids=true | all-gather | bytes 163840 | tf_op jit(solution)/shard_map/all_gather | solution.py:121
  198.6 3.8 %fusion.63 = f32[64,2048]{1,0:T(8,128)} fusion(bf16[64,1024]{1,0:T(8,128)(2,1)S(1)} %all_gather.7, bf16[1024,2048]{1,0:T(8,128)(2,1)} %param.17), kind=kOutput, calls=%fused_computation.122 | convolution fusion | flops 268435456 | bytes 4849664 | tf_op jit(solution)/shard_map/dot_general | solution.py:120
  202.5 51.1 %all-reduce.7.cloned.1.call-done = f32[64,2048]{1,0:T(8,128)} async-done(((f32[64,2048]{1,0:T(8,128)}), f32[64,2048]{1,0:T(8,128)}) %all-reduce.7.cloned.1.call-update) | async-done | bytes 524304 | tf_op jit(solution)/shard_map/psum | solution.py:125
  (87 shorter events, 20.2 us)
Async XLA Ops:
  6.5 5.5 %copy-start = (bf16[2048,256]{1,0:T(8,128)(2,1)S(1)}, bf16[2048,256]{1,0:T(8,128)(2,1)}, u32[]{:S(2)}) copy-start(bf16[2048,256]{1,0:T(8,128)(2,1)} %param.16) | copy-start | bytes 3145732
  6.5 37.6 %reduce-scatter.3.cloned.1.call-start = ((), (), s32[]{:S(2)}) async-start(), calls=%async_computation.6 | async-start | bytes 409600 | tf_op jit(solution)/shard_map/reduce_scatter | solution.py:93
  16.5 19.3 %copy-start.1 = (s32[64]{0:T(128)S(1)}, s32[64]{0:T(128)}, u32[]{:S(2)}) copy-start(s32[64]{0:T(128)} %param.19) | copy-start | bytes 772
  16.5 20.1 %copy-start.2 = (u32[32]{0:T(128)S(1)}, u32[32]{0:T(128)}, u32[]{:S(2)}) copy-start(u32[32]{0:T(128)} %constant.56) | copy-start | bytes 388
  45.8 8.8 %all-to-all-start = ((f32[8,2,1280]{2,1,0:T(2,128)}), f32[8,2,1280]{2,1,0:T(2,128)S(1)}, u32[]{:S(2)}, u32[]{:S(2)}) async-start(f32[8,2,1280]{2,1,0:T(2,128)} %all_to_all.52), calls=%async_computation.1 | async-start | bytes 163840 | tf_op jit(solution)/shard_map/all_to_all | solution.py:97
  49.5 86.2 %all-reduce.5.cloned.1.call-start = ((), (), s32[]{:S(2)}) async-start(), calls=%async_computation.7 | async-start | bytes 1048576 | tf_op jit(solution)/shard_map/psum | solution.py:125
  84.5 76.1 %reduce-scatter.5.cloned.1.call-start = ((), (), s32[]{:S(2)}) async-start(), calls=%async_computation.8 | async-start | bytes 409600 | tf_op jit(solution)/shard_map/reduce_scatter | solution.py:93
  162.3 8.8 %all-to-all-start.2 = ((f32[8,2,1280]{2,1,0:T(2,128)}), f32[8,2,1280]{2,1,0:T(2,128)S(1)}, u32[]{:S(2)}, u32[]{:S(2)}) async-start(f32[8,2,1280]{2,1,0:T(2,128)} %all_to_all.59), calls=%async_computation.4 | async-start | bytes 163840 | tf_op jit(solution)/shard_map/all_to_all | solution.py:97
  176.9 8.1 %all-to-all-start.3 = ((bf16[2,8,1024]{2,0,1:T(2,128)(2,1)}), bf16[2,8,1024]{2,0,1:T(2,128)(2,1)S(1)}, u32[]{:S(2)}, u32[]{:S(2)}) async-start(bf16[2,8,1024]{2,0,1:T(2,128)(2,1)} %copy.24), calls=%async_computation.5 | async-start | bytes 65536 | tf_op jit(solution)/shard_map/all_to_all | solution.py:119
  180.3 73.2 %all-reduce.7.cloned.1.call-start = ((), (), s32[]{:S(2)}) async-start(), calls=%async_computation.9 | async-start | bytes 1048576 | tf_op jit(solution)/shard_map/psum | solution.py:125
Sparse Core Ops, SparseCore 0:
  16.4 22.8 reduce-scatter.2
  84.7 50.9 all-reduce.4
  141.2 19.3 reduce-scatter.4
  202.6 50.9 all-reduce.6
where the time goes:
time: 264 us; the launch traced here: 263 us
  waiting for transfers between devices  124 us (47%)
  blocking collectives  59.3 us (22%)
  matrix products  23.7 us (9%)
  local copies, waits for them, and re-layouts  20.5 us (8%)
  between operations  14.1 us (5%)
  starting transfers between devices  10.8 us (4%)
  other arithmetic  10.4 us (4%)
    psum x2, waiting for transfers between devices, shards(): totals = lax.psum(partial_out, 'mp')  102 us
    all_gather x2, blocking collectives, shards(): lax.all_gather(returned, 'dp', axis=0, tiled=True)  27 us
    unnamed x2, blocking collectives  25.1 us
    all_to_all x2, waiting for transfers between devices, shards(): lax.all_to_all(projected, 'mp', split_axis=0, concat_axis=1, tiled=True)  9.31 us
    reduce_scatter x2, waiting for transfers between devices, shards(): lax.psum_scatter(partial_value, 'dp', scatter_dimension=0, tiled=True)  7.74 us
    dot_general x2, matrix products, shards(): jnp.dot(lax.all_gather(returned, 'dp', axis=0, tiled=True), w_out, prefer...  7.69 us
    all_to_all x2, starting transfers between devices, shards(): lax.all_to_all(projected, 'mp', split_axis=0, concat_axis=1, tiled=True)  7.36 us
    all_to_all x1, blocking collectives, shards(): lax.all_to_all(attended, 'mp', split_axis=1, concat_axis=0, tiled=True)  7.22 us
  transfers between devices with their start and end apart: 7, of which 6 were waited for; matrix products, arithmetic and copies ran while one was open for 6% of the time, Pallas kernels for 0%

commit v1 on v0

--- a/solution.py
+++ b/solution.py
@@ -1,3 +1,4 @@
+import functools
 import math
 import jax
 import jax.numpy as jnp
@@ -7,6 +8,15 @@
 LAYERS = 2
 norm_eps = 1e-05
 rope_base = 500000.0
+
+
+def name_views_all(local_x, row_dim, array_axis):
+    seen_now = jnp.split(local_x, lax.axis_size("mp"), axis=row_dim)
+    w1 = lax.all_to_all(jnp.stack(seen_now, axis=0), axis_name="mp", split_axis=0, concat_axis=0)
+    return jnp.concatenate(w1, axis=array_axis)
+
+
+enter_the_orders = functools.partial(name_views_all, row_dim=0, array_axis=1)
 
 
 def rotate(values, at_positions):
@@ -94,7 +104,7 @@
         square_sum = lax.psum_scatter(squares, "dp", scatter_dimension=0, tiled=True)
         inverse_rms = lax.rsqrt(square_sum / model_width + norm_eps)
         projected = summed * inverse_rms[:, None]
-        arrived = lax.all_to_all(projected, "mp", split_axis=0, concat_axis=1, tiled=True)
+        arrived = enter_the_orders(projected)
         arrived = arrived.reshape(owned_rows, model_count, projected.shape[1])
         query_part = arrived[:, :, :query_cols].reshape(owned_rows, head_count, head_dim)
         keyval_part = arrived[:, :, query_cols:].reshape(owned_rows, 2 * half_width)

time: 264 us -> 272 us (1.030)
  local copies, waits for them, and re-layouts: 20.5 us -> 28.7 us
    unnamed x13 -> x27, local copies, waits for them, and re-layouts: 0.62 us -> 9.06 us
  transfers between devices with their start and end apart: 7 -> 7, of which waited for: 6 -> 6; matrix products, arithmetic and copies ran while one was open for 6% -> 5% of each run, Pallas kernels for 0% -> 0%
where the time goes in v1:
time: 272 us; the launch traced here: 271 us
  waiting for transfers between devices  124 us (46%)
  blocking collectives  59.5 us (22%)
  local copies, waits for them, and re-layouts  28.7 us (11%)
  matrix products  23.7 us (9%)
  between operations  14.1 us (5%)
  starting transfers between devices  10.8 us (4%)
  other arithmetic  10.4 us (4%)
    psum x2, waiting for transfers between devices, shards(): totals = lax.psum(partial_out, 'mp')  102 us
    all_gather x2, blocking collectives, shards(): lax.all_gather(returned, 'dp', axis=0, tiled=True)  27.2 us
    unnamed x2, blocking collectives  25.1 us
    all_to_all x2, waiting for transfers between devices, name_views_all(): lax.all_to_all(jnp.stack(seen_now, axis=0), axis_name='mp', split_axis=0,...  9.31 us
    unnamed x27, local copies, waits for them, and re-layouts  9.06 us
    reduce_scatter x2, waiting for transfers between devices, shards(): lax.psum_scatter(partial_value, 'dp', scatter_dimension=0, tiled=True)  7.74 us
    dot_general x2, matrix products, shards(): jnp.dot(lax.all_gather(returned, 'dp', axis=0, tiled=True), w_out, prefer...  7.69 us
    all_to_all x2, starting transfers between devices, name_views_all(): lax.all_to_all(jnp.stack(seen_now, axis=0), axis_name='mp', split_axis=0,...  7.36 us
  transfers between devices with their start and end apart: 7, of which 6 were waited for; matrix products, arithmetic and copies ran while one was open for 5% of the time, Pallas kernels for 0%

profile of v1, /device:TPU:0, one launch (start us, length us, event | category | flops | bytes accessed | tf_op | source)
XLA Modules:
  0.0 271.2 jit_solution(6451374794084236256)
XLA Ops:
  12.4 3.1 %fusion.30 = f32[64,1024]{1,0:T(8,128)S(1)} fusion(bf16[2048,1024]{1,0:T(8,128)(2,1)} %param.15, f32[2048]{0:T(1024)S(1)} %convert_element_type.90, bf16[64,2048]{1,0:T(8,128)(2,1)S(1)} %gather_fusion, pred[64]{0:T(512)(128)(4,1)S(1)} %get-tuple-element.10), kind=kOutput, calls=%fused_computation.50 | convolution fusion | flops 268959744 | bytes 4726848 | tf_op jit(solution)/shard_map/dot_general | solution.py:98
  16.5 5.9 %fusion.59 = (bf16[1,2,2,8,512,128]{5,4,3,2,1,0:T(8,128)(2,1)}, bf16[1,2,2,8,512,128]{5,4,3,2,1,0:T(8,128)(2,1)}) fusion(bf16[2,2,2,8,512,128]{5,4,3,2,1,0:T(8,128)(2,1)} %param.18), kind=kLoop, calls=%fused_computation.150 | loop fusion | bytes 16777216 | tf_op jit(solution)/shard_map/slice | solution.py:124
  22.4 13.4 %all-reduce = f32[64]{0:T(128)S(1)} all-reduce(f32[64]{0:T(128)S(1)} %fusion.15), channel_id=3, replica_groups=mesh['dp'=4,'mp'=8] {'dp'}, use_global_device_ids=true, to_apply=%region_2.0.clone | all-reduce | flops 64 | bytes 512
  38.2 5.9 %copy_bitcast_fusion = (bf16[2,2,8,512,128]{4,3,2,0,1:T(8,128)(2,1)}, bf16[2,2,8,512,128]{4,3,2,0,1:T(8,128)(2,1)}) fusion(bf16[1,2,2,8,512,128]{5,4,3,2,1,0:T(8,128)(2,1)} %get-tuple-element.12, bf16[1,2,2,8,512,128]{5,4,3,2,1,0:T(8,128)(2,1)} %get-tuple-element.11), kind=kLoop, calls=%fused_computation.5 | loop fusion | bytes 16777216 | tf_op jit(solution)/shard_map/squeeze | solution.py:124
  50.0 3.7 %all-to-all-start = ((f32[8,2,1280]{2,1,0:T(2,128)}), f32[8,2,1280]{2,1,0:T(2,128)S(1)}, u32[]{:S(2)}, u32[]{:S(2)}) async-start(f32[8,2,1280]{2,1,0:T(2,128)} %constant_dynamic-update-slice_fusion), calls=%async_computation.1 | async-start | bytes 163840 | tf_op jit(solution)/shard_map/all_to_all | solution.py:15
  53.8 5.0 %all-to-all-done = f32[8,2,1280]{2,1,0:T(2,128)S(1)} async-done(((f32[8,2,1280]{2,1,0:T(2,128)}), f32[8,2,1280]{2,1,0:T(2,128)S(1)}, u32[]{:S(2)}, u32[]{:S(2)}) %all-to-all-start) | async-done | bytes 81952 | tf_op jit(solution)/shard_map/all_to_all | solution.py:15
  59.3 2.4 fusion.60
  62.0 2.0 fusion.13
  64.1 7.2 %all_to_all.48 = bf16[2,8,1024]{2,0,1:T(2,128)(2,1)S(1)} all-to-all(bf16[2,8,1024]{2,0,1:T(2,128)(2,1)S(1)} %copy.20), channel_id=1, replica_groups=mesh['dp'=4,'mp'=8] {'mp'}, dimensions={1} | all-to-all | bytes 65536 | tf_op jit(solution)/shard_map/all_to_all | solution.py:129
  71.3 13.5 %all_gather.6 = bf16[64,1024]{1,0:T(8,128)(2,1)S(1)} all-gather(bf16[16,1024]{1,0:T(8,128)(2,1)S(1)} %all_to_all.38), channel_id=1, replica_groups=mesh['dp'=4,'mp'=8] {'dp'}, dimensions={0}, use_global_device_ids=true | all-gather | bytes 163840 | tf_op jit(solution)/shard_map/all_gather | solution.py:131
  84.8 3.8 %fusion.62 = f32[64,2048]{1,0:T(8,128)} fusion(bf16[64,1024]{1,0:T(8,128)(2,1)S(1)} %all_gather.6, bf16[1024,2048]{1,0:T(8,128)(2,1)} %param.17), kind=kOutput, calls=%fused_computation.153 | convolution fusion | flops 268435456 | bytes 4849664 | tf_op jit(solution)/shard_map/dot_general | solution.py:130
  88.7 51.1 %all-reduce.5.cloned.1.call-done = f32[64,2048]{1,0:T(8,128)} async-done(((f32[64,2048]{1,0:T(8,128)}), f32[64,2048]{1,0:T(8,128)}) %all-reduce.5.cloned.1.call-update) | async-done | bytes 524304 | tf_op jit(solution)/shard_map/psum | solution.py:135
  141.4 3.0 %fusion.26 = f32[64,1024]{1,0:T(8,128)S(1)} fusion(bf16[2048,1024]{1,0:T(8,128)(2,1)} %param.15, bf16[64,2048]{1,0:T(8,128)(2,1)S(1)} %get-tuple-element.8, f32[2048]{0:T(1024)S(1)} %convert_element_type.90), kind=kOutput, calls=%fused_computation.48 | convolution fusion | flops 268828672 | bytes 4726784 | tf_op jit(solution)/shard_map/dot_general | solution.py:98
  145.3 11.7 %all-reduce.1 = f32[64]{0:T(128)S(1)} all-reduce(f32[64]{0:T(128)S(1)} %get-tuple-element.6), channel_id=5, replica_groups=mesh['dp'=4,'mp'=8] {'dp'}, use_global_device_ids=true, to_apply=%region_8.11.clone | all-reduce | flops 64 | bytes 512
  157.0 7.7 %reduce-scatter.5.cloned.1.call-done = f32[16,1280]{1,0:T(8,128)} async-done(((f32[64,1280]{1,0:T(8,128)}), f32[16,1280]{1,0:T(8,128)}) %reduce-scatter.5.cloned.1.call-update) | async-done | bytes 81936 | tf_op jit(solution)/shard_map/reduce_scatter | solution.py:103
  170.6 3.7 %all-to-all-start.2 = ((f32[8,2,1280]{2,1,0:T(2,128)}), f32[8,2,1280]{2,1,0:T(2,128)S(1)}, u32[]{:S(2)}, u32[]{:S(2)}) async-start(f32[8,2,1280]{2,1,0:T(2,128)} %constant_dynamic-update-slice_fusion.8), calls=%async_computation.4 | async-start | bytes 163840 | tf_op jit(solution)/shard_map/all_to_all | solution.py:15
  175.0 4.3 %all-to-all-done.2 = f32[8,2,1280]{2,1,0:T(2,128)S(1)} async-done(((f32[8,2,1280]{2,1,0:T(2,128)}), f32[8,2,1280]{2,1,0:T(2,128)S(1)}, u32[]{:S(2)}, u32[]{:S(2)}) %all-to-all-start.2) | async-done | bytes 81952 | tf_op jit(solution)/shard_map/all_to_all | solution.py:15
  179.7 2.4 fusion.61
  182.5 2.0 fusion.12
  185.2 3.3 %all-to-all-start.3 = ((bf16[2,8,1024]{2,0,1:T(2,128)(2,1)}), bf16[2,8,1024]{2,0,1:T(2,128)(2,1)S(1)}, u32[]{:S(2)}, u32[]{:S(2)}) async-start(bf16[2,8,1024]{2,0,1:T(2,128)(2,1)} %copy.23), calls=%async_computation.5 | async-start | bytes 65536 | tf_op jit(solution)/shard_map/all_to_all | solution.py:129
  188.6 4.7 %all-to-all-done.3 = bf16[2,8,1024]{2,0,1:T(2,128)(2,1)S(1)} async-done(((bf16[2,8,1024]{2,0,1:T(2,128)(2,1)}), bf16[2,8,1024]{2,0,1:T(2,128)(2,1)S(1)}, u32[]{:S(2)}, u32[]{:S(2)}) %all-to-all-start.3) | async-done | bytes 32800 | tf_op jit(solution)/shard_map/all_to_all | solution.py:129
  193.4 13.6 %all_gather.7 = bf16[64,1024]{1,0:T(8,128)(2,1)S(1)} all-gather(bf16[16,1024]{1,0:T(8,128)(2,1)S(1)} %all_to_all.43), channel_id=1, replica_groups=mesh['dp'=4,'mp'=8] {'dp'}, dimensions={0}, use_global_device_ids=true | all-gather | bytes 163840 | tf_op jit(solution)/shard_map/all_gather | solution.py:131
  207.0 3.8 %fusion.63 = f32[64,2048]{1,0:T(8,128)} fusion(bf16[64,1024]{1,0:T(8,128)(2,1)S(1)} %all_gather.7, bf16[1024,2048]{1,0:T(8,128)(2,1)} %param.17), kind=kOutput, calls=%fused_computation.154 | convolution fusion | flops 268435456 | bytes 4849664 | tf_op jit(solution)/shard_map/dot_general | solution.py:130
  210.9 51.1 %all-reduce.7.cloned.1.call-done = f32[64,2048]{1,0:T(8,128)} async-done(((f32[64,2048]{1,0:T(8,128)}), f32[64,2048]{1,0:T(8,128)}) %all-reduce.7.cloned.1.call-update) | async-done | bytes 524304 | tf_op jit(solution)/shard_map/psum | solution.py:135
  (101 shorter events, 28.5 us)
Async XLA Ops:
  6.5 5.5 %copy-start = (bf16[2048,256]{1,0:T(8,128)(2,1)S(1)}, bf16[2048,256]{1,0:T(8,128)(2,1)}, u32[]{:S(2)}) copy-start(bf16[2048,256]{1,0:T(8,128)(2,1)} %param.16) | copy-start | bytes 3145732
  6.5 37.6 %reduce-scatter.3.cloned.1.call-start = ((), (), s32[]{:S(2)}) async-start(), calls=%async_computation.6 | async-start | bytes 409600 | tf_op jit(solution)/shard_map/reduce_scatter | solution.py:103
  16.5 19.3 %copy-start.1 = (s32[64]{0:T(128)S(1)}, s32[64]{0:T(128)}, u32[]{:S(2)}) copy-start(s32[64]{0:T(128)} %param.19) | copy-start | bytes 772
  16.5 20.1 %copy-start.2 = (u32[32]{0:T(128)S(1)}, u32[32]{0:T(128)}, u32[]{:S(2)}) copy-start(u32[32]{0:T(128)} %constant.56) | copy-start | bytes 388
  50.0 8.8 %all-to-all-start = ((f32[8,2,1280]{2,1,0:T(2,128)}), f32[8,2,1280]{2,1,0:T(2,128)S(1)}, u32[]{:S(2)}, u32[]{:S(2)}) async-start(f32[8,2,1280]{2,1,0:T(2,128)} %constant_dynamic-update-slice_fusion), calls=%async_computation.1 | async-start | bytes 163840 | tf_op jit(solution)/shard_map/all_to_all | solution.py:15
  53.7 86.2 %all-reduce.5.cloned.1.call-start = ((), (), s32[]{:S(2)}) async-start(), calls=%async_computation.7 | async-start | bytes 1048576 | tf_op jit(solution)/shard_map/psum | solution.py:135
  88.7 76.1 %reduce-scatter.5.cloned.1.call-start = ((), (), s32[]{:S(2)}) async-start(), calls=%async_computation.8 | async-start | bytes 409600 | tf_op jit(solution)/shard_map/reduce_scatter | solution.py:103
  170.6 8.8 %all-to-all-start.2 = ((f32[8,2,1280]{2,1,0:T(2,128)}), f32[8,2,1280]{2,1,0:T(2,128)S(1)}, u32[]{:S(2)}, u32[]{:S(2)}) async-start(f32[8,2,1280]{2,1,0:T(2,128)} %constant_dynamic-update-slice_fusion.8), calls=%async_computation.4 | async-start | bytes 163840 | tf_op jit(solution)/shard_map/all_to_all | solution.py:15
  185.2 8.1 %all-to-all-start.3 = ((bf16[2,8,1024]{2,0,1:T(2,128)(2,1)}), bf16[2,8,1024]{2,0,1:T(2,128)(2,1)S(1)}, u32[]{:S(2)}, u32[]{:S(2)}) async-start(bf16[2,8,1024]{2,0,1:T(2,128)(2,1)} %copy.23), calls=%async_computation.5 | async-start | bytes 65536 | tf_op jit(solution)/shard_map/all_to_all | solution.py:129
  188.6 73.4 %all-reduce.7.cloned.1.call-start = ((), (), s32[]{:S(2)}) async-start(), calls=%async_computation.9 | async-start | bytes 1048576 | tf_op jit(solution)/shard_map/psum | solution.py:135
Sparse Core Ops, SparseCore 0:
  16.4 22.8 reduce-scatter.2
  88.8 50.9 all-reduce.4
  145.4 19.3 reduce-scatter.4
  211.0 50.9 all-reduce.6
